TPU v7x, 512 devices: a whole 4x8x8 slice. The times are simulated.
512 devices in a mesh: pair: 16 (over z, core), virt: 32 (over x, y).
Axes of the slice: x: 4, y: 8, z: 8, core: 2. Of those that a mesh axis runs over, the one named last changes fastest.
Arguments:
- amplitudes: bfloat16 [1024, 512, 512], P('pair', 'virt')
- integrals: bfloat16 [8, 512, 512, 512], P(None, 'pair', 'virt')
- pair_occ: int32 [1024, 2], P('virt'), may hold values from 0 to 119, as said below
- occ_irrep: int32 [120], replicated, may hold values from 0 to 7, as said below
- virt_irrep: int32 [512], replicated, may hold values from 0 to 7, as said below
- occ_energy: float32 [120], replicated, may hold values from -3 to -0.5
- virt_energy: float32 [512], replicated, may hold values from 0.3 to 4
Outputs:
- update: float32 [1024, 8, 512], P('virt', None, 'pair')
Inputs may be any that keep to these rules, and one draw needn't show every extreme that they name: `pair_occ`: each row holds i < j, and rows are distinct. `occ_irrep`: labels of the D2h irreps; every label occurs. `virt_irrep`: labels of the D2h irreps; every label occurs.
All inputs are finite; a program needn't handle non-finite values.
Results may differ from a plain program's by a relative error of at most 0.0003.
Values may be sent and summed in bfloat16 or wider, within the bound.
A program may use at most 128 MiB of HBM per device.

v0:
```python
import jax
import jax.numpy as jnp
from jax import lax
from jax.sharding import PartitionSpec as P


def table_lookup(indices, table, zero_value):
    orbital = jnp.arange(table.shape[0], dtype=jnp.int32)
    hits = indices[:, None] == orbital[None, :]
    return jnp.sum(jnp.where(hits, table[None, :], zero_value), axis=1)


def local(amplitudes, integrals, pair_occ, occ_irrep, virt_irrep, occ_energy, virt_energy):
    window_size, local_width, local_depth, full_width = integrals.shape
    integral_matrix = integrals.reshape(window_size * local_width, local_depth * full_width)
    owned_rows = pair_occ.shape[0]
    block_rows = lax.all_gather(amplitudes, "pair", axis=0, tiled=True)
    flattened = block_rows.reshape(block_rows.shape[0], local_depth * full_width)
    partial_value = lax.dot_general(
        flattened, integral_matrix, (((1,), (1,)), ((), ())), preferred_element_type=jnp.float32
    )
    summed = lax.psum(partial_value, "virt")
    ladder = lax.dynamic_slice_in_dim(summed, lax.axis_index("virt") * owned_rows, owned_rows, 0)
    ladder = ladder.reshape(owned_rows, window_size, local_width)
    b_offset = lax.axis_index("pair") * local_width
    local_sym = lax.dynamic_slice_in_dim(virt_irrep, b_offset, local_width, 0)
    local_energy = lax.dynamic_slice_in_dim(virt_energy, b_offset, local_width, 0)
    first_occ = pair_occ[:, 0]
    second_occ = pair_occ[:, 1]
    pair_sym = jnp.bitwise_xor(
        table_lookup(first_occ, occ_irrep, 0), table_lookup(second_occ, occ_irrep, 0)
    )
    pair_energy = table_lookup(first_occ, occ_energy, 0.0) + table_lookup(
        second_occ, occ_energy, 0.0
    )
    window_sym = virt_irrep[:window_size]
    total_sym = jnp.bitwise_xor(
        pair_sym[:, None, None],
        jnp.bitwise_xor(window_sym[None, :, None], local_sym[None, None, :]),
    )
    allowed = total_sym == 0
    denom = (
        pair_energy[:, None, None]
        - virt_energy[:window_size][None, :, None]
        - local_energy[None, None, :]
    )
    return jnp.where(allowed, ladder / denom, jnp.zeros_like(ladder))


def solution(mesh):
    return jax.shard_map(
        local,
        mesh=mesh,
        in_specs=(
            P("pair", "virt", None),
            P(None, "pair", "virt", None),
            P("virt", None),
            P(),
            P(),
            P(),
            P(),
        ),
        out_specs=P("virt", None, "pair"),
        check_vma=False,
    )
```

profile of v0, /device:TPU:64, one launch (start us, length us, event | category | flops | bytes accessed | tf_op | source)
XLA Modules:
  0.0 301.6 jit_solution(1929621240613633479)
XLA Ops:
  6.5 0.0 all-gather.2.cloned.1.call-start
  6.5 0.7 all-gather.2.cloned.1.call-update
  7.3 0.0 all-reduce.2.cloned.1.call-start
  7.3 8.4 %copy.9 = bf16[32,8,16,512]{3,1,2,0:T(8,128)(2,1)} copy(bf16[32,8,16,512]{3,2,1,0:T(8,128)(2,1)} %bitcast.13) | data formatting | bytes 8388608
  15.7 94.0 %all-gather.2.cloned.1.call-done = bf16[1024,16,512]{2,1,0:T(8,128)(2,1)} async-done(((bf16[64,16,512]{2,1,0:T(8,128)(2,1)}), bf16[1024,16,512]{2,1,0:T(8,128)(2,1)}) %all-gather.2.cloned.1.call-update) | async-done | bytes 16777232 | tf_op jit(solution)/shard_map/all_gather | solution.py:17
  109.7 0.0 copy-start
  109.7 16.0 %copy.8 = bf16[128,8,16,512]{3,1,2,0:T(8,128)(2,1)S(1)} copy(bf16[128,8,16,512]{3,2,1,0:T(8,128)(2,1)} %bitcast.11) | data formatting | bytes 33554432
  125.7 0.0 copy-start.4
  125.7 0.0 copy-start.5
  125.7 0.0 copy-start.1
  125.8 0.0 copy-start.2
  125.8 0.0 copy-start.3
  125.8 0.0 slice-start.1
  125.8 0.0 slice-start
  125.8 0.0 copy-done
  125.8 5.5 %fusion = f32[1024,256]{1,0:T(8,128)} fusion(bf16[1024,8192]{1,0:T(8,128)(2,1)S(1)} %bitcast.12, bf16[256,8192]{1,0:T(8,128)(2,1)S(1)} %bitcast.14), kind=kOutput, calls=%fused_computation.13 | convolution fusion | flops 4294967296 | bytes 22020096 | tf_op jit(solution)/shard_map/dot_general | solution.py:19
  131.4 0.0 all-reduce.2.cloned.1.call-update
  131.4 0.0 copy-done.4
  131.4 0.1 dynamic_slice.11
  131.5 0.0 copy-done.5
  131.5 0.1 dynamic_slice.9
  131.5 0.0 copy-done.1
  131.6 0.0 copy-done.2
  131.6 0.2 select_reduce_fusion
  131.8 0.0 copy-done.3
  131.8 0.2 select_reduce_fusion.2
  132.0 0.0 slice-done.1
  132.0 0.1 broadcast_xor_fusion
  132.0 0.0 slice-done
  132.0 0.1 broadcast_subtract_fusion
  132.1 161.0 %all-reduce.2.cloned.1.call-done = f32[1024,256]{1,0:T(8,128)} async-done(((f32[1024,256]{1,0:T(8,128)}), f32[1024,256]{1,0:T(8,128)}) %all-reduce.2.cloned.1.call-update) | async-done | bytes 1048592 | tf_op jit(solution)/shard_map/psum | solution.py:22
  293.1 0.8 constant_dynamic-slice_fusion
  293.9 0.1 reshape.87
  294.0 0.8 divide_select_fusion
  (3 shorter events, 0.0 us)
Async XLA Ops:
  6.5 103.2 %all-gather.2.cloned.1.call-start = ((), (), s32[]{:S(2)}) async-start(), calls=%async_computation | async-start | bytes 17825792 | tf_op jit(solution)/shard_map/all_gather | solution.py:17
  7.3 285.9 %all-reduce.2.cloned.1.call-start = ((), (), s32[]{:S(2)}) async-start(), calls=%async_computation.1 | async-start | bytes 2097152 | tf_op jit(solution)/shard_map/psum | solution.py:22
  109.7 16.1 %copy-start = (bf16[32,8,16,512]{3,1,2,0:T(8,128)(2,1)S(1)}, bf16[32,8,16,512]{3,1,2,0:T(8,128)(2,1)}, u32[]{:S(2)}) copy-start(bf16[32,8,16,512]{3,1,2,0:T(8,128)(2,1)} %copy.9) | copy-start | bytes 12582916
  125.7 5.7 %copy-start.4 = (f32[512]{0:T(512)S(1)}, f32[512]{0:T(512)}, u32[]{:S(2)}) copy-start(f32[512]{0:T(512)} %param.13) | copy-start | bytes 6148
  125.7 5.7 %copy-start.5 = (s32[512]{0:T(512)S(1)}, s32[512]{0:T(512)}, u32[]{:S(2)}) copy-start(s32[512]{0:T(512)} %param.11) | copy-start | bytes 6148
  125.7 5.8 %copy-start.1 = (s32[32,2]{0,1:T(2,128)S(1)}, s32[32,2]{0,1:T(2,128)}, u32[]{:S(2)}) copy-start(s32[32,2]{0,1:T(2,128)} %param.9) | copy-start | bytes 772
  125.8 5.8 %copy-start.2 = (f32[120]{0:T(128)S(1)}, f32[120]{0:T(128)}, u32[]{:S(2)}) copy-start(f32[120]{0:T(128)} %param.12) | copy-start | bytes 1444
  125.8 6.0 %copy-start.3 = (s32[120]{0:T(128)S(1)}, s32[120]{0:T(128)}, u32[]{:S(2)}) copy-start(s32[120]{0:T(128)} %param.10) | copy-start | bytes 1444
  125.8 6.2 %slice-start.1 = ((s32[512]{0:T(512)}), s32[8]{0:T(128)S(1)}, s32[]{:S(2)}) async-start(s32[512]{0:T(512)} %param.11), calls=%async_computation.3 | async-start | bytes 1024 | tf_op jit(solution)/shard_map/slice | solution.py:36
  125.8 6.2 %slice-start = ((f32[512]{0:T(512)}), f32[8]{0:T(128)S(1)}, s32[]{:S(2)}) async-start(f32[512]{0:T(512)} %param.13), calls=%async_computation.2 | async-start | bytes 1024 | tf_op jit(solution)/shard_map/slice | solution.py:44
Sparse Core Ops, SparseCore 0:
  9.4 100.2 all-gather.1
  131.5 161.6 all-reduce.1
where the time goes:
time: 302 us
  waiting for transfers between devices  256 us (85%)
  local copies, waits for them, and re-layouts  25.5 us (8%)
  between operations  13.5 us (4%)
  matrix products  5.53 us (2%)
    psum x1, waiting for transfers between devices, local(): summed = lax.psum(partial_value, 'virt')  161 us
    all_gather x1, waiting for transfers between devices, local(): block_rows = lax.all_gather(amplitudes, 'pair', axis=0, tiled=True)  94 us
    unnamed x14, local copies, waits for them, and re-layouts  24.5 us
  transfers between devices with their start and end apart: 2, of which 2 were waited for; matrix products, arithmetic and copies ran while one was open for 3% of the time, Pallas kernels for 0%

commit v1 on v0

--- a/solution.py
+++ b/solution.py
@@ -14,7 +14,9 @@
     window_size, local_width, local_depth, full_width = integrals.shape
     integral_matrix = integrals.reshape(window_size * local_width, local_depth * full_width)
     owned_rows = pair_occ.shape[0]
-    block_rows = lax.all_gather(amplitudes, "pair", axis=0, tiled=True)
+    block_rows = jnp.concatenate(
+        lax.all_to_all(jnp.stack([amplitudes] * lax.axis_size("pair")), "pair", 0, 0), axis=0
+    )
     flattened = block_rows.reshape(block_rows.shape[0], local_depth * full_width)
     partial_value = lax.dot_general(
         flattened, integral_matrix, (((1,), (1,)), ((), ())), preferred_element_type=jnp.float32

time: 302 us -> 578 us (1.91)
  waiting for transfers between devices: 256 us -> 515 us
  starting transfers between devices: 0.04 us -> 10 us
  local copies, waits for them, and re-layouts: 25.5 us -> 32.4 us
    all_to_all x0 -> x1, waiting for transfers between devices: none -> 354 us  [local(): lax.all_to_all(jnp.stack([amplitudes] * lax.axis_size('pair')), 'pair', 0...]
    all_gather x1 -> x0, waiting for transfers between devices: 94 us -> none  [local(): block_rows = lax.all_gather(amplitudes, 'pair', axis=0, tiled=True)]
    all_to_all x0 -> x1, starting transfers between devices: none -> 9.98 us  [local(): lax.all_to_all(jnp.stack([amplitudes] * lax.axis_size('pair')), 'pair', 0...]
    another operation x0 -> x1, local copies, waits for them, and re-layouts: none -> 6.84 us  [local(): jnp.stack([amplitudes] * lax.axis_size('pair'))]
  transfers between devices with their start and end apart: 2 -> 2, of which waited for: 2 -> 2; matrix products, arithmetic and copies ran while one was open for 3% -> 2% of each run, Pallas kernels for 0% -> 0%
where the time goes in v1:
time: 578 us
  waiting for transfers between devices  515 us (89%)
  local copies, waits for them, and re-layouts  32.4 us (6%)
  between operations  13.5 us (2%)
  starting transfers between devices  10 us (2%)
    all_to_all x1, waiting for transfers between devices, local(): lax.all_to_all(jnp.stack([amplitudes] * lax.axis_size('pair')), 'pair', 0...  354 us
    psum x1, waiting for transfers between devices, local(): summed = lax.psum(partial_value, 'virt')  161 us
    unnamed x14, local copies, waits for them, and re-layouts  24.6 us
  transfers between devices with their start and end apart: 2, of which 2 were waited for; matrix products, arithmetic and copies ran while one was open for 2% of the time, Pallas kernels for 0%

profile of v1, /device:TPU:64, one launch (start us, length us, event | category | flops | bytes accessed | tf_op | source)
XLA Modules:
  0.0 577.8 jit_solution(1644711326187701061)
XLA Ops:
  6.5 6.8 %stack.2 = bf16[16,64,16,512]{3,2,1,0:T(8,128)(2,1)} broadcast(bf16[64,16,512]{2,1,0:T(8,128)(2,1)} %param.7), dimensions={1,2,3} | broadcast | bytes 17825792 | tf_op jit(solution)/shard_map/stack | solution.py:18
  13.4 10.0 %all-to-all-start = ((bf16[16,64,16,512]{3,2,1,0:T(8,128)(2,1)}), bf16[16,64,16,512]{3,2,1,0:T(8,128)(2,1)}, u32[]{:S(2)}, u32[]{:S(2)}) async-start(bf16[16,64,16,512]{3,2,1,0:T(8,128)(2,1)} %stack.2), calls=%async_computation | async-start | bytes 33554432 | tf_op jit(solution)/shard_map/all_to_all | solution.py:18
  23.4 0.0 all-reduce.2.cloned.1.call-start
  23.4 8.5 %copy.9 = bf16[32,8,16,512]{3,1,2,0:T(8,128)(2,1)} copy(bf16[32,8,16,512]{3,2,1,0:T(8,128)(2,1)} %bitcast.13) | data formatting | bytes 8388608
  31.9 354.2 %all-to-all-done = bf16[16,64,16,512]{3,2,1,0:T(8,128)(2,1)} async-done(((bf16[16,64,16,512]{3,2,1,0:T(8,128)(2,1)}), bf16[16,64,16,512]{3,2,1,0:T(8,128)(2,1)}, u32[]{:S(2)}, u32[]{:S(2)}) %all-to-all-start) | async-done | bytes 16777248 | tf_op jit(solution)/shard_map/all_to_all | solution.py:18
  386.1 0.0 copy-start
  386.2 16.0 %copy.8 = bf16[128,8,16,512]{3,1,2,0:T(8,128)(2,1)S(1)} copy(bf16[128,8,16,512]{3,2,1,0:T(8,128)(2,1)} %bitcast.3) | data formatting | bytes 33554432
  402.2 0.0 copy-start.4
  402.2 0.0 copy-start.5
  402.2 0.0 copy-start.1
  402.2 0.0 copy-start.2
  402.2 0.0 copy-start.3
  402.2 0.0 slice-start.1
  402.2 0.0 slice-start
  402.2 0.0 copy-done
  402.2 5.5 fusion
  407.8 0.0 all-reduce.2.cloned.1.call-update
  407.8 0.0 copy-done.4
  407.8 0.1 dynamic_slice.11
  407.9 0.0 copy-done.5
  407.9 0.1 dynamic_slice.9
  408.0 0.0 copy-done.1
  408.0 0.0 copy-done.2
  408.0 0.2 select_reduce_fusion
  408.2 0.0 copy-done.3
  408.2 0.2 select_reduce_fusion.2
  408.4 0.0 slice-done.1
  408.4 0.1 broadcast_xor_fusion
  408.5 0.0 slice-done
  408.5 0.1 broadcast_subtract_fusion
  408.6 160.8 %all-reduce.2.cloned.1.call-done = f32[1024,256]{1,0:T(8,128)} async-done(((f32[1024,256]{1,0:T(8,128)}), f32[1024,256]{1,0:T(8,128)}) %all-reduce.2.cloned.1.call-update) | async-done | bytes 1048592 | tf_op jit(solution)/shard_map/psum | solution.py:24
  569.3 0.8 constant_dynamic-slice_fusion
  570.1 0.1 reshape.85
  570.2 0.8 divide_select_fusion
  (3 shorter events, 0.0 us)
Async XLA Ops:
  13.4 372.8 %all-to-all-start = ((bf16[16,64,16,512]{3,2,1,0:T(8,128)(2,1)}), bf16[16,64,16,512]{3,2,1,0:T(8,128)(2,1)}, u32[]{:S(2)}, u32[]{:S(2)}) async-start(bf16[16,64,16,512]{3,2,1,0:T(8,128)(2,1)} %stack.2), calls=%async_computation | async-start | bytes 33554432 | tf_op jit(solution)/shard_map/all_to_all | solution.py:18
  23.4 546.0 %all-reduce.2.cloned.1.call-start = ((), (), s32[]{:S(2)}) async-start(), calls=%async_computation.1 | async-start | bytes 2097152 | tf_op jit(solution)/shard_map/psum | solution.py:24
  386.1 16.1 %copy-start = (bf16[32,8,16,512]{3,1,2,0:T(8,128)(2,1)S(1)}, bf16[32,8,16,512]{3,1,2,0:T(8,128)(2,1)}, u32[]{:S(2)}) copy-start(bf16[32,8,16,512]{3,1,2,0:T(8,128)(2,1)} %copy.9) | copy-start | bytes 12582916
  402.2 5.7 copy-start.4
  402.2 5.7 copy-start.5
  402.2 5.8 %copy-start.1 = (s32[32,2]{0,1:T(2,128)S(1)}, s32[32,2]{0,1:T(2,128)}, u32[]{:S(2)}) copy-start(s32[32,2]{0,1:T(2,128)} %param.9) | copy-start | bytes 772
  402.2 5.8 %copy-start.2 = (f32[120]{0:T(128)S(1)}, f32[120]{0:T(128)}, u32[]{:S(2)}) copy-start(f32[120]{0:T(128)} %param.12) | copy-start | bytes 1444
  402.2 6.0 %copy-start.3 = (s32[120]{0:T(128)S(1)}, s32[120]{0:T(128)}, u32[]{:S(2)}) copy-start(s32[120]{0:T(128)} %param.10) | copy-start | bytes 1444
  402.2 6.2 %slice-start.1 = ((s32[512]{0:T(512)}), s32[8]{0:T(128)S(1)}, s32[]{:S(2)}) async-start(s32[512]{0:T(512)} %param.11), calls=%async_computation.3 | async-start | bytes 1024 | tf_op jit(solution)/shard_map/slice | solution.py:38
  402.2 6.3 %slice-start = ((f32[512]{0:T(512)}), f32[8]{0:T(128)S(1)}, s32[]{:S(2)}) async-start(f32[512]{0:T(512)} %param.13), calls=%async_computation.2 | async-start | bytes 1024 | tf_op jit(solution)/shard_map/slice | solution.py:46
Sparse Core Ops, SparseCore 0:
  407.9 161.3 all-reduce.1

commit v2 on v0

--- a/solution.py
+++ b/solution.py
@@ -19,7 +19,9 @@
     partial_value = lax.dot_general(
         flattened, integral_matrix, (((1,), (1,)), ((), ())), preferred_element_type=jnp.float32
     )
-    summed = lax.psum(partial_value, "virt")
+    summed = partial_value
+    for hop in (1, 2, 4, 8, 16):
+        summed = summed + lax.ppermute(summed, "virt", [(dev, dev ^ hop) for dev in range(32)])
     ladder = lax.dynamic_slice_in_dim(summed, lax.axis_index("virt") * owned_rows, owned_rows, 0)
     ladder = ladder.reshape(owned_rows, window_size, local_width)
     b_offset = lax.axis_index("pair") * local_width

time: 302 us -> 325 us (1.076)
  the two profiles are of different devices: /device:TPU:64 before, /device:TPU:26 now
where the time goes in v2:
time: 325 us
  waiting for transfers between devices  264 us (81%)
  local copies, waits for them, and re-layouts  24.7 us (8%)
  starting transfers between devices  16 us (5%)
  between operations  13.6 us (4%)
  matrix products  4.53 us (1%)
    ppermute x5, waiting for transfers between devices, local(): lax.ppermute(summed, 'virt', [(dev, dev ^ hop) for dev in range(32)])  167 us
    all_gather x1, waiting for transfers between devices, local(): block_rows = lax.all_gather(amplitudes, 'pair', axis=0, tiled=True)  96.9 us
    unnamed x14, local copies, waits for them, and re-layouts  24.5 us
    ppermute x5, starting transfers between devices, local(): lax.ppermute(summed, 'virt', [(dev, dev ^ hop) for dev in range(32)])  16 us
  transfers between devices with their start and end apart: 6, of which 6 were waited for; matrix products, arithmetic and copies ran while one was open for 3% of the time, Pallas kernels for 0%

profile of v2, /device:TPU:26, one launch (start us, length us, event | category | flops | bytes accessed | tf_op | source)
XLA Modules:
  0.0 324.9 jit_solution(14396882831817059738)
XLA Ops:
  6.5 0.0 all-gather.2.cloned.1.call-start
  6.5 0.7 all-gather.2.cloned.1.call-update
  7.3 8.4 %copy.9 = bf16[32,8,16,512]{3,1,2,0:T(8,128)(2,1)} copy(bf16[32,8,16,512]{3,2,1,0:T(8,128)(2,1)} %bitcast.13) | data formatting | bytes 8388608
  15.7 96.9 %all-gather.2.cloned.1.call-done = bf16[1024,16,512]{2,1,0:T(8,128)(2,1)} async-done(((bf16[64,16,512]{2,1,0:T(8,128)(2,1)}), bf16[1024,16,512]{2,1,0:T(8,128)(2,1)}) %all-gather.2.cloned.1.call-update) | async-done | bytes 16777232 | tf_op jit(solution)/shard_map/all_gather | solution.py:17
  112.6 0.0 copy-start
  112.6 16.0 %copy.8 = bf16[128,8,16,512]{3,1,2,0:T(8,128)(2,1)S(1)} copy(bf16[128,8,16,512]{3,2,1,0:T(8,128)(2,1)} %bitcast.11) | data formatting | bytes 33554432
  128.6 0.0 copy-done
  128.6 0.0 copy-start.5
  128.7 0.0 copy-start.4
  128.7 0.0 copy-start.1
  128.7 0.0 copy-start.2
  128.7 0.0 copy-start.3
  128.7 0.0 slice-start.1
  128.7 0.0 slice-start
  128.7 4.5 %fusion = f32[1024,256]{1,0:T(8,128)S(1)} fusion(bf16[1024,8192]{1,0:T(8,128)(2,1)S(1)} %bitcast.12, bf16[256,8192]{1,0:T(8,128)(2,1)S(1)} %bitcast.14), kind=kOutput, calls=%fused_computation.13 | convolution fusion | flops 4294967296 | bytes 22020096 | tf_op jit(solution)/shard_map/dot_general | solution.py:19
  133.3 2.4 collective-permute-start
  135.7 24.8 %collective-permute-done = f32[1024,256]{1,0:T(8,128)S(1)} collective-permute-done((f32[1024,256]{1,0:T(8,128)S(1)}, f32[1024,256]{1,0:T(8,128)S(1)}, u32[]{:S(2)}, u32[]{:S(2)}) %collective-permute-start) | collective-permute-done | bytes 1048608 | tf_op jit(solution)/shard_map/ppermute | solution.py:24
  160.5 0.1 add.30
  160.6 2.4 collective-permute-start.1
  163.0 47.3 %collective-permute-done.1 = f32[1024,256]{1,0:T(8,128)S(1)} collective-permute-done((f32[1024,256]{1,0:T(8,128)S(1)}, f32[1024,256]{1,0:T(8,128)S(1)}, u32[]{:S(2)}, u32[]{:S(2)}) %collective-permute-start.1) | collective-permute-done | bytes 1048608 | tf_op jit(solution)/shard_map/ppermute | solution.py:24
  210.3 0.1 add.31
  210.4 4.7 %collective-permute-start.2 = (f32[1024,256]{1,0:T(8,128)S(1)}, f32[1024,256]{1,0:T(8,128)S(1)}, u32[]{:S(2)}, u32[]{:S(2)}) collective-permute-start(f32[1024,256]{1,0:T(8,128)S(1)} %add.31), channel_id=1, source_target_pairs={{0,4},{1,5},{2,6},{3,7},{4,0},{5,1},{6,2},{7,3},{8,12},{9,13},{10,... | collective-permute-start | bytes 3145736 | tf_op jit(solution)/shard_map/ppermute | solution.py:24
  215.1 47.2 %collective-permute-done.2 = f32[1024,256]{1,0:T(8,128)S(1)} collective-permute-done((f32[1024,256]{1,0:T(8,128)S(1)}, f32[1024,256]{1,0:T(8,128)S(1)}, u32[]{:S(2)}, u32[]{:S(2)}) %collective-permute-start.2) | collective-permute-done | bytes 1048608 | tf_op jit(solution)/shard_map/ppermute | solution.py:24
  262.4 0.1 add.32
  262.5 2.5 collective-permute-start.3
  265.0 24.5 %collective-permute-done.3 = f32[1024,256]{1,0:T(8,128)S(1)} collective-permute-done((f32[1024,256]{1,0:T(8,128)S(1)}, f32[1024,256]{1,0:T(8,128)S(1)}, u32[]{:S(2)}, u32[]{:S(2)}) %collective-permute-start.3) | collective-permute-done | bytes 1048608 | tf_op jit(solution)/shard_map/ppermute | solution.py:24
  289.4 0.1 add.33
  289.6 4.0 %collective-permute-start.4 = (f32[1024,256]{1,0:T(8,128)S(1)}, f32[1024,256]{1,0:T(8,128)S(1)}, u32[]{:S(2)}, u32[]{:S(2)}) collective-permute-start(f32[1024,256]{1,0:T(8,128)S(1)} %add.33), channel_id=1, source_target_pairs={{0,16},{1,17},{2,18},{3,19},{4,20},{5,21},{6,22},{7,23},{8,24},{9,... | collective-permute-start | bytes 3145736 | tf_op jit(solution)/shard_map/ppermute | solution.py:24
  293.6 0.0 copy-done.5
  293.6 0.1 dynamic_slice.9
  293.7 0.0 copy-done.4
  293.7 0.1 dynamic_slice.11
  293.7 0.0 copy-done.1
  293.7 0.0 copy-done.2
  293.8 0.2 select_reduce_fusion
  293.9 0.0 copy-done.3
  294.0 0.2 select_reduce_fusion.2
  294.1 0.0 slice-done.1
  294.2 0.1 broadcast_xor_fusion
  294.2 0.0 slice-done
  294.2 0.1 broadcast_subtract_fusion
  294.3 22.9 %collective-permute-done.4 = f32[1024,256]{1,0:T(8,128)S(1)} collective-permute-done((f32[1024,256]{1,0:T(8,128)S(1)}, f32[1024,256]{1,0:T(8,128)S(1)}, u32[]{:S(2)}, u32[]{:S(2)}) %collective-permute-start.4) | collective-permute-done | bytes 1048608 | tf_op jit(solution)/shard_map/ppermute | solution.py:24
  317.2 0.1 reshape.87
  317.3 0.8 divide_select_fusion
  (4 shorter events, 0.0 us)
Async XLA Ops:
  6.5 106.1 %all-gather.2.cloned.1.call-start = ((), (), s32[]{:S(2)}) async-start(), calls=%async_computation | async-start | bytes 17825792 | tf_op jit(solution)/shard_map/all_gather | solution.py:17
  112.6 16.0 %copy-start = (bf16[32,8,16,512]{3,1,2,0:T(8,128)(2,1)S(1)}, bf16[32,8,16,512]{3,1,2,0:T(8,128)(2,1)}, u32[]{:S(2)}) copy-start(bf16[32,8,16,512]{3,1,2,0:T(8,128)(2,1)} %copy.9) | copy-start | bytes 12582916
  128.6 164.9 %copy-start.5 = (s32[512]{0:T(512)S(1)}, s32[512]{0:T(512)}, u32[]{:S(2)}) copy-start(s32[512]{0:T(512)} %param.11) | copy-start | bytes 6148
  128.7 165.0 %copy-start.4 = (f32[512]{0:T(512)S(1)}, f32[512]{0:T(512)}, u32[]{:S(2)}) copy-start(f32[512]{0:T(512)} %param.13) | copy-start | bytes 6148
  128.7 165.1 %copy-start.1 = (s32[32,2]{0,1:T(2,128)S(1)}, s32[32,2]{0,1:T(2,128)}, u32[]{:S(2)}) copy-start(s32[32,2]{0,1:T(2,128)} %param.9) | copy-start | bytes 772
  128.7 165.1 %copy-start.2 = (f32[120]{0:T(128)S(1)}, f32[120]{0:T(128)}, u32[]{:S(2)}) copy-start(f32[120]{0:T(128)} %param.12) | copy-start | bytes 1444
  128.7 165.3 %copy-start.3 = (s32[120]{0:T(128)S(1)}, s32[120]{0:T(128)}, u32[]{:S(2)}) copy-start(s32[120]{0:T(128)} %param.10) | copy-start | bytes 1444
  128.7 165.4 %slice-start.1 = ((s32[512]{0:T(512)}), s32[8]{0:T(128)S(1)}, s32[]{:S(2)}) async-start(s32[512]{0:T(512)} %param.11), calls=%async_computation.2 | async-start | bytes 1024 | tf_op jit(solution)/shard_map/slice | solution.py:38
  128.7 165.5 %slice-start = ((f32[512]{0:T(512)}), f32[8]{0:T(128)S(1)}, s32[]{:S(2)}) async-start(f32[512]{0:T(512)} %param.13), calls=%async_computation.1 | async-start | bytes 1024 | tf_op jit(solution)/shard_map/slice | solution.py:46
  133.3 27.2 %collective-permute-start = (f32[1024,256]{1,0:T(8,128)S(1)}, f32[1024,256]{1,0:T(8,128)S(1)}, u32[]{:S(2)}, u32[]{:S(2)}) collective-permute-start(f32[1024,256]{1,0:T(8,128)S(1)} %fusion), channel_id=1, source_target_pairs={{0,1},{1,0},{2,3},{3,2},{4,5},{5,4},{6,7},{7,6},{8,9},{9,8},{10,11... | collective-permute-start | bytes 3145736 | tf_op jit(solution)/shard_map/ppermute | solution.py:24
  160.6 49.7 %collective-permute-start.1 = (f32[1024,256]{1,0:T(8,128)S(1)}, f32[1024,256]{1,0:T(8,128)S(1)}, u32[]{:S(2)}, u32[]{:S(2)}) collective-permute-start(f32[1024,256]{1,0:T(8,128)S(1)} %add.30), channel_id=1, source_target_pairs={{0,2},{1,3},{2,0},{3,1},{4,6},{5,7},{6,4},{7,5},{8,10},{9,11},{10,... | collective-permute-start | bytes 3145736 | tf_op jit(solution)/shard_map/ppermute | solution.py:24
  210.4 51.9 %collective-permute-start.2 = (f32[1024,256]{1,0:T(8,128)S(1)}, f32[1024,256]{1,0:T(8,128)S(1)}, u32[]{:S(2)}, u32[]{:S(2)}) collective-permute-start(f32[1024,256]{1,0:T(8,128)S(1)} %add.31), channel_id=1, source_target_pairs={{0,4},{1,5},{2,6},{3,7},{4,0},{5,1},{6,2},{7,3},{8,12},{9,13},{10,... | collective-permute-start | bytes 3145736 | tf_op jit(solution)/shard_map/ppermute | solution.py:24
  262.5 26.9 %collective-permute-start.3 = (f32[1024,256]{1,0:T(8,128)S(1)}, f32[1024,256]{1,0:T(8,128)S(1)}, u32[]{:S(2)}, u32[]{:S(2)}) collective-permute-start(f32[1024,256]{1,0:T(8,128)S(1)} %add.32), channel_id=1, source_target_pairs={{0,8},{1,9},{2,10},{3,11},{4,12},{5,13},{6,14},{7,15},{8,0},{9,1},... | collective-permute-start | bytes 3145736 | tf_op jit(solution)/shard_map/ppermute | solution.py:24
  289.6 27.6 %collective-permute-start.4 = (f32[1024,256]{1,0:T(8,128)S(1)}, f32[1024,256]{1,0:T(8,128)S(1)}, u32[]{:S(2)}, u32[]{:S(2)}) collective-permute-start(f32[1024,256]{1,0:T(8,128)S(1)} %add.33), channel_id=1, source_target_pairs={{0,16},{1,17},{2,18},{3,19},{4,20},{5,21},{6,22},{7,23},{8,24},{9,... | collective-permute-start | bytes 3145736 | tf_op jit(solution)/shard_map/ppermute | solution.py:24
Sparse Core Ops, SparseCore 0:
  9.4 103.1 all-gather.1
